TPU v7x, 32 devices: a whole 2x2x4 slice. The times are simulated.
32 devices in a mesh: expert: 16 (over z, y, x), loop: 2 (over core).
Axes of the slice: x: 2, y: 2, z: 4, core: 2. Of those that a mesh axis runs over, the one named last changes fastest.
Arguments:
- tokens: bfloat16 [2048, 7168], P('expert', 'loop'), may hold values from -6 to 6
- expert_ids: int32 [2048, 8], P('expert'), may hold values from 0 to 255, all different within a row; in each aligned block of 128 rows (0 to 127, 128 to 255, ...) at most 8 rows name the same one
- route_weights: float32 [2048, 8], P('expert'), may hold values from 0.1 to 1
- up_proj: bfloat16 [16, 7168, 1024], P('expert', None, 'loop'), may hold values from -0.0625 to 0.0625
- down_proj: bfloat16 [16, 1024, 7168], P('expert', None, 'loop'), may hold values from -0.1875 to 0.1875
Outputs:
- combined: bfloat16 [2048, 7168], P('expert', 'loop')
Inputs may be any that keep to these rules, and one draw needn't show every extreme that they name: `expert_ids`: each row names 8 different experts. Among the 128 rows held by one device along `expert`, no expert is chosen by more than 8 rows, a bound that some block reaches.
All inputs are finite; a program needn't handle non-finite values.
Results may differ from a plain program's by a relative error of at most 0.0058.
Values may be sent and summed in bfloat16 or wider, within the bound.
No kernel may reach another device: no remote copies, remote signals or barrier semaphores. Data moves between devices by JAX's collectives and lax.ppermute only.
A program may use at most 64 MiB of HBM per device.

v0:
```python
import jax
import jax.numpy as jnp
from jax import lax
from jax.sharding import PartitionSpec as P


def slot_tables(expert_ids, route_weights, flight, capacity):
    tok_count = expert_ids.shape[0]
    experts = jnp.arange(flight, dtype=jnp.int32)
    matches = expert_ids[:, :, None] == experts[None, None, :]
    chosen = jnp.any(matches, axis=1)
    weight = jnp.sum(jnp.where(matches, route_weights[:, :, None], 0.0), axis=1)
    ranking = jnp.cumsum(chosen.astype(jnp.int32), axis=0) - 1
    places = jnp.arange(capacity, dtype=jnp.int32)
    picked = chosen[:, :, None] & (ranking[:, :, None] == places[None, None, :])
    tok_index = jnp.arange(tok_count, dtype=jnp.int32)
    slot_token = jnp.sum(jnp.where(picked, tok_index[:, None, None], 0), axis=0).reshape(
        flight * capacity
    )
    slot_weight = jnp.sum(jnp.where(picked, weight[:, :, None], 0.0), axis=0).reshape(
        flight * capacity
    )
    slot_live = jnp.any(picked, axis=0).reshape(flight * capacity)
    return (slot_token, slot_weight, slot_live)


def on_device(tokens, expert_ids, route_weights, up_proj, down_proj):
    tok_rows = tokens.shape[0]
    capacity = tok_rows // 16
    owners = lax.axis_size("expert")
    per_owner = up_proj.shape[0]
    flight = owners * per_owner
    slot_count = owners * capacity
    slot_token, slot_weight, slot_live = slot_tables(expert_ids, route_weights, flight, capacity)
    live_mask = slot_live.astype(jnp.bfloat16)[:, None]
    features = lax.all_gather(tokens, "loop", axis=1, tiled=True)
    full_width = features.shape[1]
    outgoing = (jnp.take(features, slot_token, axis=0) * live_mask).reshape(
        owners, per_owner * capacity, full_width
    )
    arrived = lax.all_to_all(outgoing, "expert", split_axis=0, concat_axis=0, tiled=True)
    slot_rows = (
        arrived.reshape(owners, per_owner, capacity, full_width)
        .transpose(1, 0, 2, 3)
        .reshape(per_owner, slot_count, full_width)
    )
    up_sums = jnp.einsum("esd,edh->esh", slot_rows, up_proj, preferred_element_type=jnp.float32)
    hidden = jax.nn.silu(up_sums).astype(jnp.bfloat16)
    out_width = down_proj.shape[2]
    out_rows = jnp.einsum(
        "esh,ehd->esd",
        lax.all_gather(hidden, "loop", axis=2, tiled=True),
        down_proj,
        preferred_element_type=jnp.float32,
    ).astype(jnp.bfloat16)
    homeward = (
        out_rows.reshape(per_owner, owners, capacity, out_width)
        .transpose(1, 0, 2, 3)
        .reshape(owners, per_owner * capacity, out_width)
    )
    returned = lax.all_to_all(homeward, "expert", split_axis=0, concat_axis=0, tiled=True).reshape(
        flight * capacity, out_width
    )
    scaled = slot_weight[:, None] * returned.astype(jnp.float32)
    combined = jax.ops.segment_sum(scaled, slot_token, num_segments=tok_rows)
    return combined.astype(jnp.bfloat16)


def solution(mesh):
    return jax.shard_map(
        on_device,
        mesh=mesh,
        in_specs=(
            P("expert", "loop"),
            P("expert", None),
            P("expert", None),
            P("expert", None, "loop"),
            P("expert", None, "loop"),
        ),
        out_specs=P("expert", "loop"),
        check_vma=False,
    )
```

profile of v0, /device:TPU:0, one launch (start us, length us, event | category | flops | bytes accessed | tf_op | source)
XLA Modules:
  0.0 124.3 jit_solution(4287521138012820241)
XLA Ops:
  6.5 0.7 all-gather.3.cloned.1.call-update
  7.3 0.7 fusion.20
  8.0 0.1 copy.10
  8.1 0.2 reduce_window_sum.11
  8.3 0.1 copy.11
  8.3 0.4 select_reduce_fusion.2
  8.7 0.1 broadcast_in_dim_reshape.4
  8.8 0.4 fusion.22
  9.2 12.6 %all-gather.3.cloned.1.call-done = bf16[128,7168]{1,0:T(8,128)(2,1)} async-done(((bf16[128,3584]{1,0:T(8,128)(2,1)}), bf16[128,7168]{1,0:T(8,128)(2,1)}) %all-gather.3.cloned.1.call-update) | async-done | bytes 1835024 | tf_op jit(solution)/shard_map/all_gather | solution.py:36
  21.8 5.1 %gather_fusion = bf16[128,7168]{1,0:T(8,128)(2,1)S(1)} fusion(bf16[128,7168]{1,0:T(8,128)(2,1)} %all-gather.3.cloned.1.call-done, s32[1024]{0:T(1024)S(1)} %pad_clamp_fusion), kind=kCustom, calls=%fused_computation | custom fusion | bytes 3670528 | tf_op jit(solution)/shard_map/jit(_take)/gather | solution.py:38
  26.9 0.2 fusion.12
  27.2 0.0 slice-start
  27.2 51.1 %all_to_all.10 = bf16[16,8,7168]{2,1,0:T(8,128)(2,1)S(1)} all-to-all(bf16[16,8,7168]{2,1,0:T(8,128)(2,1)S(1)} %fusion.12), channel_id=1, replica_groups=mesh['expert'=16,'loop'=2] {'expert'}, dimensions={0} | all-to-all | bytes 3670016 | tf_op jit(solution)/shard_map/all_to_all | solution.py:41
  78.3 4.4 %multiply_convert_fusion = bf16[128,512]{1,0:T(8,128)(2,1)S(1)} fusion(bf16[1,7168,512]{2,1,0:T(8,128)(2,1)} %param.8, bf16[16,8,7168]{2,1,0:T(8,128)(2,1)S(1)} %all_to_all.10), kind=kOutput, calls=%fused_computation.16 | convolution fusion | flops 939851776 | bytes 9306112 | tf_op jit(solution)/shard_map/esd,edh->esh/dot_general | solution.py:47
  82.7 2.0 %all-gather = bf16[128,1024]{1,0:T(8,128)(2,1)S(1)} all-gather(bf16[128,512]{1,0:T(8,128)(2,1)S(1)} %multiply_convert_fusion), channel_id=2, replica_groups=mesh['expert'=16,'loop'=2] {'loop'}, dimensions={1}, use_global_device_ids=true | all-gather | bytes 393216 | tf_op jit(solution)/shard_map/all_gather | solution.py:52
  84.7 0.0 slice-done
  84.7 2.1 %fusion.7 = bf16[16,8,3584]{2,1,0:T(8,128)(2,1)} fusion(bf16[128,1024]{1,0:T(8,128)(2,1)S(1)} %all-gather, bf16[1,1024,3584]{2,1,0:T(8,128)(2,1)S(1)} %bitcast.33), kind=kOutput, calls=%fused_computation.7 | convolution fusion | flops 939982848 | bytes 8519680 | tf_op jit(solution)/shard_map/esh,ehd->esd/dot_general | solution.py:50
  86.7 3.8 %all-to-all-start.1 = ((bf16[16,8,3584]{2,1,0:T(8,128)(2,1)}), bf16[16,8,3584]{2,1,0:T(8,128)(2,1)S(1)}, u32[]{:S(2)}, u32[]{:S(2)}) async-start(bf16[16,8,3584]{2,1,0:T(8,128)(2,1)} %fusion.7), calls=%async_computation.1 | async-start | bytes 1835008 | tf_op jit(solution)/shard_map/all_to_all | solution.py:61
  90.5 0.1 reshape.106
  90.6 0.1 select_reduce_fusion
  90.7 0.1 mul.24
  90.8 22.0 %all-to-all-done.1 = bf16[16,8,3584]{2,1,0:T(8,128)(2,1)S(1)} async-done(((bf16[16,8,3584]{2,1,0:T(8,128)(2,1)}), bf16[16,8,3584]{2,1,0:T(8,128)(2,1)S(1)}, u32[]{:S(2)}, u32[]{:S(2)}) %all-to-all-start.1) | async-done | bytes 917536 | tf_op jit(solution)/shard_map/all_to_all | solution.py:61
  112.8 3.6 %scatter_custom_fusion = f32[128,3584]{1,0:T(8,128)S(1)} fusion(s32[128]{0:T(128)S(1)} %reshape.106, bf16[16,8,3584]{2,1,0:T(8,128)(2,1)S(1)} %all-to-all-done.1, f32[128]{0:T(128)S(1)} %mul.24, f32[]{:T(128)} %constant.11.clone.1), kind=kCustom, calls=%fused_computation.9 | custom fusion | flops 1376256 | bytes 2753028 | tf_op jit(solution)/shard_map/scatter-add | solution.py:65
  116.4 1.0 convert_element_type.40
  (15 shorter events, 0.1 us)
Async XLA Ops:
  6.5 15.3 %all-gather.3.cloned.1.call-start = ((), (), s32[]{:S(2)}) async-start(), calls=%async_computation.2 | async-start | bytes 2752512 | tf_op jit(solution)/shard_map/all_gather | solution.py:36
  27.2 57.5 %slice-start = ((s8[7340032]{0:T(1024)(128)(4,1)}), s8[4194304]{0:T(1024)(128)(4,1)S(1)}, s32[]{:S(2)}) async-start(s8[7340032]{0:T(1024)(128)(4,1)} %bitcast.32), calls=%async_computation.3 | async-start | bytes 8388608
  78.3 6.4 %slice-start.1 = ((s8[7340032]{0:T(1024)(128)(4,1)}), s8[3145728]{0:T(1024)(128)(4,1)S(1)}, s32[]{:S(2)}) async-start(s8[7340032]{0:T(1024)(128)(4,1)} %bitcast.32), calls=%async_computation.4 | async-start | bytes 6291456
  86.7 3.9 %copy-start = (s32[128,8]{0,1:T(8,128)S(1)}, s32[128,8]{0,1:T(8,128)}, u32[]{:S(2)}) copy-start(s32[128,8]{0,1:T(8,128)} %param.6) | copy-start | bytes 12292
  86.7 3.9 %copy-start.1 = (f32[128,8]{0,1:T(8,128)S(1)}, f32[128,8]{0,1:T(8,128)}, u32[]{:S(2)}) copy-start(f32[128,8]{0,1:T(8,128)} %param.7) | copy-start | bytes 12292
  86.7 26.1 %all-to-all-start.1 = ((bf16[16,8,3584]{2,1,0:T(8,128)(2,1)}), bf16[16,8,3584]{2,1,0:T(8,128)(2,1)S(1)}, u32[]{:S(2)}, u32[]{:S(2)}) async-start(bf16[16,8,3584]{2,1,0:T(8,128)(2,1)} %fusion.7), calls=%async_computation.1 | async-start | bytes 1835008 | tf_op jit(solution)/shard_map/all_to_all | solution.py:61
Sparse Core Ops, SparseCore 0:
  8.9 12.8 all-gather.2
where the time goes:
time: 125 us; the launch traced here: 124 us
  blocking collectives  53.1 us (42%)
  waiting for transfers between devices  35.3 us (28%)
  between operations  13.5 us (11%)
  other arithmetic  6.58 us (5%)
  matrix products  6.47 us (5%)
  local copies, waits for them, and re-layouts  5.53 us (4%)
  starting transfers between devices  3.77 us (3%)
    all_to_all x1, blocking collectives, on_device(): lax.all_to_all(outgoing, 'expert', split_axis=0, concat_axis=0, tiled=True)  51.1 us
    all_to_all x1, waiting for transfers between devices, on_device(): lax.all_to_all(homeward, 'expert', split_axis=0, concat_axis=0, tiled=True)  22 us
    all_gather x1, waiting for transfers between devices, on_device(): features = lax.all_gather(tokens, 'loop', axis=1, tiled=True)  12.6 us
    gather x1, local copies, waits for them, and re-layouts, on_device(): jnp.take(features, slot_token, axis=0) * live_mask  5.1 us
    dot_general x1, matrix products, on_device(): jnp.einsum('esd,edh->esh', slot_rows, up_proj, preferred_element_type=jnp...  4.4 us
    all_to_all x1, starting transfers between devices, on_device(): lax.all_to_all(homeward, 'expert', split_axis=0, concat_axis=0, tiled=True)  3.77 us
    scatter-add x1, other arithmetic, on_device(): combined = jax.ops.segment_sum(scaled, slot_token, num_segments=tok_rows)  3.58 us
  transfers between devices with their start and end apart: 2, of which 2 were waited for; matrix products, arithmetic and copies ran while one was open for 2% of the time, Pallas kernels for 0%

commit v1 on v0

--- a/solution.py
+++ b/solution.py
@@ -2,6 +2,29 @@
 import jax.numpy as jnp
 from jax import lax
 from jax.sharding import PartitionSpec as P
+
+
+def in_blocks(value, dim, length):
+    before, after = (value.shape[:dim], value.shape[dim + 1 :])
+    return jnp.moveaxis(value.reshape(*before, length, -1, *after), dim, 0)
+
+
+def laid_out(tiles, dim):
+    tiles = jnp.moveaxis(tiles, 0, dim)
+    shape = tiles.shape
+    return tiles.reshape(*shape[:dim], shape[dim] * shape[dim + 1], *shape[dim + 2 :])
+
+
+def rotated_exchange(shard, axis, split_dim, concat_dim):
+    peers, index = (lax.axis_size(axis), lax.axis_index(axis))
+    parts = in_blocks(shard, split_dim, peers)
+    filled = parts
+    for step in range(1, peers):
+        target, source = ((index + step) % peers, (index - step) % peers)
+        sent = lax.dynamic_index_in_dim(parts, target, 0)
+        other = lax.ppermute(sent, axis, [(i, (i + step) % peers) for i in range(peers)])
+        filled = lax.dynamic_update_slice_in_dim(filled, other, source, axis=0)
+    return laid_out(filled, concat_dim)
 
 
 def slot_tables(expert_ids, route_weights, flight, capacity):
@@ -38,7 +61,7 @@
     outgoing = (jnp.take(features, slot_token, axis=0) * live_mask).reshape(
         owners, per_owner * capacity, full_width
     )
-    arrived = lax.all_to_all(outgoing, "expert", split_axis=0, concat_axis=0, tiled=True)
+    arrived = rotated_exchange(outgoing, "expert", 0, 0)
     slot_rows = (
         arrived.reshape(owners, per_owner, capacity, full_width)
         .transpose(1, 0, 2, 3)

time: 125 us -> 166 us (1.33)
  waiting for transfers between devices: 35.3 us -> 104 us
  blocking collectives: 53.1 us -> 1.99 us
  starting transfers between devices: 3.77 us -> 23.7 us
  local copies, waits for them, and re-layouts: 5.53 us -> 7.8 us
    ppermute x0 -> x15, waiting for transfers between devices: none -> 68.4 us  [rotated_exchange(): lax.ppermute(sent, axis, [(i, (i + step) % peers) for i in range(peers)])]
    all_to_all x1 -> x0, blocking collectives: 51.1 us -> none  [on_device(): lax.all_to_all(outgoing, 'expert', split_axis=0, concat_axis=0, tiled=True)]
    ppermute x0 -> x15, starting transfers between devices: none -> 14.4 us  [rotated_exchange(): lax.ppermute(sent, axis, [(i, (i + step) % peers) for i in range(peers)])]
    all_to_all x1, starting transfers between devices: 3.77 us -> 9.26 us  [on_device(): lax.all_to_all(homeward, 'expert', split_axis=0, concat_axis=0, tiled=True)]
  transfers between devices with their start and end apart: 2 -> 17, of which waited for: 2 -> 13; matrix products, arithmetic and copies ran while one was open for 2% -> 1% of each run, Pallas kernels for 0% -> 0%
where the time goes in v1:
time: 166 us; the launch traced here: 165 us
  waiting for transfers between devices  104 us (63%)
  starting transfers between devices  23.7 us (14%)
  between operations  13.7 us (8%)
  other arithmetic  8.08 us (5%)
  local copies, waits for them, and re-layouts  7.8 us (5%)
  matrix products  6.47 us (4%)
  blocking collectives  1.99 us (1%)
    ppermute x15, waiting for transfers between devices, rotated_exchange(): lax.ppermute(sent, axis, [(i, (i + step) % peers) for i in range(peers)])  68.4 us
    all_to_all x1, waiting for transfers between devices, on_device(): lax.all_to_all(homeward, 'expert', split_axis=0, concat_axis=0, tiled=True)  22 us
    ppermute x15, starting transfers between devices, rotated_exchange(): lax.ppermute(sent, axis, [(i, (i + step) % peers) for i in range(peers)])  14.4 us
    all_gather x1, waiting for transfers between devices, on_device(): features = lax.all_gather(tokens, 'loop', axis=1, tiled=True)  12.6 us
    all_to_all x1, starting transfers between devices, on_device(): lax.all_to_all(homeward, 'expert', split_axis=0, concat_axis=0, tiled=True)  9.26 us
    gather x1, local copies, waits for them, and re-layouts, on_device(): jnp.take(features, slot_token, axis=0) * live_mask  6.33 us
    dot_general x1, matrix products, on_device(): jnp.einsum('esd,edh->esh', slot_rows, up_proj, preferred_element_type=jnp...  4.41 us
    scatter-add x1, other arithmetic, on_device(): combined = jax.ops.segment_sum(scaled, slot_token, num_segments=tok_rows)  3.58 us
  transfers between devices with their start and end apart: 17, of which 13 were waited for; matrix products, arithmetic and copies ran while one was open for 1% of the time, Pallas kernels for 0%

profile of v1, /device:TPU:0, one launch (start us, length us, event | category | flops | bytes accessed | tf_op | source)
XLA Modules:
  0.0 165.4 jit_solution(5427250087384471375)
XLA Ops:
  9.2 12.6 %all-gather.3.cloned.1.call-done = bf16[128,7168]{1,0:T(8,128)(2,1)} async-done(((bf16[128,3584]{1,0:T(8,128)(2,1)}), bf16[128,7168]{1,0:T(8,128)(2,1)}) %all-gather.3.cloned.1.call-update) | async-done | bytes 1835024 | tf_op jit(solution)/shard_map/all_gather | solution.py:59
  21.8 6.3 %gather_fusion = bf16[128,7168]{1,0:T(8,128)(2,1)} fusion(bf16[128,7168]{1,0:T(8,128)(2,1)} %all-gather.3.cloned.1.call-done, s32[1024]{0:T(1024)S(1)} %pad_clamp_fusion), kind=kCustom, calls=%fused_computation | custom fusion | bytes 3670528 | tf_op jit(solution)/shard_map/jit(_take)/gather | solution.py:61
  28.2 1.7 %fusion.12 = bf16[16,1,8,7168]{3,2,0,1:T(8,128)(2,1)S(1)} fusion(bf16[128,7168]{1,0:T(8,128)(2,1)} %gather_fusion, pred[16,8]{1,0:T(8,128)(4,1)S(1)} %compare_and_fusion, bf16[16,8]{1,0:T(8,128)(2,1)S(1)} %convert_element_type.34), kind=kLoop, calls=%fused_computation.12 | loop fusion | flops 1835008 | bytes 3670400 | tf_op jit(solution)/shard_map/mul | solution.py:61
  29.9 1.8 %collective-permute-start = (bf16[1,1,8,7168]{3,2,0,1:T(8,128)(2,1)S(1)}, bf16[1,1,8,7168]{3,2,0,1:T(8,128)(2,1)S(1)}, u32[]{:S(2)}, u32[]{:S(2)}) collective-permute-start(bf16[1,1,8,7168]{3,2,0,1:T(8,128)(2,1)S(1)} %constant_dynamic-slice_fusion.14), channel_id=1, source_target_pairs={{0,2},{2,4},{4,6},{6,8},{8,10},{10,12},{12,14},{14,16},{16,18},{18... | collective-permute-start | bytes 344072 | tf_op jit(solution)/shard_map/ppermute | solution.py:25
  31.7 7.3 %collective-permute-done = bf16[1,1,8,7168]{3,2,0,1:T(8,128)(2,1)S(1)} collective-permute-done((bf16[1,1,8,7168]{3,2,0,1:T(8,128)(2,1)S(1)}, bf16[1,1,8,7168]{3,2,0,1:T(8,128)(2,1)S(1)}, u32[]{:S(2)}, u32[]{:S(2)}) %collective-permute-start) | collective-permute-done | bytes 114720 | tf_op jit(solution)/shard_map/ppermute | solution.py:25
  39.8 2.2 %collective-permute-start.14 = (bf16[1,1,8,7168]{3,2,0,1:T(8,128)(2,1)S(1)}, bf16[1,1,8,7168]{3,2,0,1:T(8,128)(2,1)S(1)}, u32[]{:S(2)}, u32[]{:S(2)}) collective-permute-start(bf16[1,1,8,7168]{3,2,0,1:T(8,128)(2,1)S(1)} %get-tuple-element.5), channel_id=1, source_target_pairs={{0,30},{2,0},{4,2},{6,4},{8,6},{10,8},{12,10},{14,12},{16,14},{18,... | collective-permute-start | bytes 344072 | tf_op jit(solution)/shard_map/ppermute | solution.py:25
  42.1 2.5 %collective-permute-start.13 = (bf16[1,1,8,7168]{3,2,0,1:T(8,128)(2,1)S(1)}, bf16[1,1,8,7168]{3,2,0,1:T(8,128)(2,1)S(1)}, u32[]{:S(2)}, u32[]{:S(2)}) collective-permute-start(bf16[1,1,8,7168]{3,2,0,1:T(8,128)(2,1)S(1)} %get-tuple-element.6), channel_id=1, source_target_pairs={{0,28},{2,30},{4,0},{6,2},{8,4},{10,6},{12,8},{14,10},{16,12},{18,... | collective-permute-start | bytes 344072 | tf_op jit(solution)/shard_map/ppermute | solution.py:25
  46.5 2.6 %collective-permute-done.1 = bf16[1,1,8,7168]{3,2,0,1:T(8,128)(2,1)S(1)} collective-permute-done((bf16[1,1,8,7168]{3,2,0,1:T(8,128)(2,1)S(1)}, bf16[1,1,8,7168]{3,2,0,1:T(8,128)(2,1)S(1)}, u32[]{:S(2)}, u32[]{:S(2)}) %collective-permute-start.1) | collective-permute-done | bytes 114720 | tf_op jit(solution)/shard_map/ppermute | solution.py:25
  49.1 7.5 %collective-permute-done.2 = bf16[1,1,8,7168]{3,2,0,1:T(8,128)(2,1)S(1)} collective-permute-done((bf16[1,1,8,7168]{3,2,0,1:T(8,128)(2,1)S(1)}, bf16[1,1,8,7168]{3,2,0,1:T(8,128)(2,1)S(1)}, u32[]{:S(2)}, u32[]{:S(2)}) %collective-permute-start.2) | collective-permute-done | bytes 114720 | tf_op jit(solution)/shard_map/ppermute | solution.py:25
  57.7 5.6 %collective-permute-done.3 = bf16[1,1,8,7168]{3,2,0,1:T(8,128)(2,1)S(1)} collective-permute-done((bf16[1,1,8,7168]{3,2,0,1:T(8,128)(2,1)}, bf16[1,1,8,7168]{3,2,0,1:T(8,128)(2,1)S(1)}, u32[]{:S(2)}, u32[]{:S(2)}) %collective-permute-start.3) | collective-permute-done | bytes 114720 | tf_op jit(solution)/shard_map/ppermute | solution.py:25
  63.4 10.2 %collective-permute-done.4 = bf16[1,1,8,7168]{3,2,0,1:T(8,128)(2,1)S(1)} collective-permute-done((bf16[1,1,8,7168]{3,2,0,1:T(8,128)(2,1)}, bf16[1,1,8,7168]{3,2,0,1:T(8,128)(2,1)S(1)}, u32[]{:S(2)}, u32[]{:S(2)}) %collective-permute-start.4) | collective-permute-done | bytes 114720 | tf_op jit(solution)/shard_map/ppermute | solution.py:25
  73.6 6.8 %collective-permute-done.5 = bf16[1,1,8,7168]{3,2,0,1:T(8,128)(2,1)S(1)} collective-permute-done((bf16[1,1,8,7168]{3,2,0,1:T(8,128)(2,1)}, bf16[1,1,8,7168]{3,2,0,1:T(8,128)(2,1)S(1)}, u32[]{:S(2)}, u32[]{:S(2)}) %collective-permute-start.5) | collective-permute-done | bytes 114720 | tf_op jit(solution)/shard_map/ppermute | solution.py:25
  80.4 7.8 %collective-permute-done.6 = bf16[1,1,8,7168]{3,2,0,1:T(8,128)(2,1)S(1)} collective-permute-done((bf16[1,1,8,7168]{3,2,0,1:T(8,128)(2,1)}, bf16[1,1,8,7168]{3,2,0,1:T(8,128)(2,1)S(1)}, u32[]{:S(2)}, u32[]{:S(2)}) %collective-permute-start.6) | collective-permute-done | bytes 114720 | tf_op jit(solution)/shard_map/ppermute | solution.py:25
  88.2 7.1 %collective-permute-done.7 = bf16[1,1,8,7168]{3,2,0,1:T(8,128)(2,1)S(1)} collective-permute-done((bf16[1,1,8,7168]{3,2,0,1:T(8,128)(2,1)S(1)}, bf16[1,1,8,7168]{3,2,0,1:T(8,128)(2,1)S(1)}, u32[]{:S(2)}, u32[]{:S(2)}) %collective-permute-start.7) | collective-permute-done | bytes 114720 | tf_op jit(solution)/shard_map/ppermute | solution.py:25
  95.4 6.6 %collective-permute-done.8 = bf16[1,1,8,7168]{3,2,0,1:T(8,128)(2,1)S(1)} collective-permute-done((bf16[1,1,8,7168]{3,2,0,1:T(8,128)(2,1)}, bf16[1,1,8,7168]{3,2,0,1:T(8,128)(2,1)S(1)}, u32[]{:S(2)}, u32[]{:S(2)}) %collective-permute-start.8) | collective-permute-done | bytes 114720 | tf_op jit(solution)/shard_map/ppermute | solution.py:25
  103.1 4.6 %collective-permute-done.9 = bf16[1,1,8,7168]{3,2,0,1:T(8,128)(2,1)S(1)} collective-permute-done((bf16[1,1,8,7168]{3,2,0,1:T(8,128)(2,1)S(1)}, bf16[1,1,8,7168]{3,2,0,1:T(8,128)(2,1)S(1)}, u32[]{:S(2)}, u32[]{:S(2)}) %collective-permute-start.9) | collective-permute-done | bytes 114720 | tf_op jit(solution)/shard_map/ppermute | solution.py:25
  107.8 3.6 %collective-permute-start.10 = (bf16[1,1,8,7168]{3,2,0,1:T(8,128)(2,1)S(1)}, bf16[1,1,8,7168]{3,2,0,1:T(8,128)(2,1)S(1)}, u32[]{:S(2)}, u32[]{:S(2)}) collective-permute-start(bf16[1,1,8,7168]{3,2,0,1:T(8,128)(2,1)S(1)} %get-tuple-element.9), channel_id=1, source_target_pairs={{0,22},{2,24},{4,26},{6,28},{8,30},{10,0},{12,2},{14,4},{16,6},{18... | collective-permute-start | bytes 344072 | tf_op jit(solution)/shard_map/ppermute | solution.py:25
  111.4 2.4 %collective-permute-done.10 = bf16[1,1,8,7168]{3,2,0,1:T(8,128)(2,1)S(1)} collective-permute-done((bf16[1,1,8,7168]{3,2,0,1:T(8,128)(2,1)S(1)}, bf16[1,1,8,7168]{3,2,0,1:T(8,128)(2,1)S(1)}, u32[]{:S(2)}, u32[]{:S(2)}) %collective-permute-start.10) | collective-permute-done | bytes 114720 | tf_op jit(solution)/shard_map/ppermute | solution.py:25
  113.9 4.4 %multiply_convert_fusion = bf16[128,512]{1,0:T(8,128)(2,1)S(1)} fusion(bf16[1,7168,512]{2,1,0:T(8,128)(2,1)} %param.8, bf16[16,1,8,7168]{3,2,0,1:T(8,128)(2,1)S(1)} %constant_dynamic-update-slice_fusion.14), kind=kOutput, calls=%fused_computation.16 | convolution fusion | flops 939851776 | bytes 9306112 | tf_op jit(solution)/shard_map/esd,edh->esh/dot_general | solution.py:70
  118.4 2.0 %all-gather = bf16[128,1024]{1,0:T(8,128)(2,1)S(1)} all-gather(bf16[128,512]{1,0:T(8,128)(2,1)S(1)} %multiply_convert_fusion), channel_id=2, replica_groups=mesh['expert'=16,'loop'=2] {'loop'}, dimensions={1}, use_global_device_ids=true | all-gather | bytes 393216 | tf_op jit(solution)/shard_map/all_gather | solution.py:75
  120.4 2.1 %fusion.7 = bf16[16,8,3584]{2,1,0:T(8,128)(2,1)} fusion(bf16[128,1024]{1,0:T(8,128)(2,1)S(1)} %all-gather, bf16[1,1024,3584]{2,1,0:T(8,128)(2,1)S(1)} %bitcast.33), kind=kOutput, calls=%fused_computation.7 | convolution fusion | flops 939982848 | bytes 8519680 | tf_op jit(solution)/shard_map/esh,ehd->esd/dot_general | solution.py:73
  122.4 9.3 %all-to-all-start = ((bf16[16,8,3584]{2,1,0:T(8,128)(2,1)}), bf16[16,8,3584]{2,1,0:T(8,128)(2,1)S(1)}, u32[]{:S(2)}, u32[]{:S(2)}) async-start(bf16[16,8,3584]{2,1,0:T(8,128)(2,1)} %fusion.7), calls=%async_computation | async-start | bytes 1835008 | tf_op jit(solution)/shard_map/all_to_all | solution.py:84
  132.0 22.0 %all-to-all-done = bf16[16,8,3584]{2,1,0:T(8,128)(2,1)S(1)} async-done(((bf16[16,8,3584]{2,1,0:T(8,128)(2,1)}), bf16[16,8,3584]{2,1,0:T(8,128)(2,1)S(1)}, u32[]{:S(2)}, u32[]{:S(2)}) %all-to-all-start) | async-done | bytes 917536 | tf_op jit(solution)/shard_map/all_to_all | solution.py:84
  154.0 3.6 %scatter_custom_fusion = f32[128,3584]{1,0:T(8,128)S(1)} fusion(s32[128]{0:T(128)S(1)} %reshape.121, bf16[16,8,3584]{2,1,0:T(8,128)(2,1)S(1)} %all-to-all-done, f32[128]{0:T(128)S(1)} %mul.30, f32[]{:T(128)} %constant.215.clone.1), kind=kCustom, calls=%fused_computation.9 | custom fusion | flops 1376256 | bytes 2753028 | tf_op jit(solution)/shard_map/scatter-add | solution.py:88
  (60 shorter events, 9.3 us)
Async XLA Ops:
  6.5 15.3 %all-gather.3.cloned.1.call-start = ((), (), s32[]{:S(2)}) async-start(), calls=%async_computation.1 | async-start | bytes 2752512 | tf_op jit(solution)/shard_map/all_gather | solution.py:59
  29.9 9.1 %collective-permute-start = (bf16[1,1,8,7168]{3,2,0,1:T(8,128)(2,1)S(1)}, bf16[1,1,8,7168]{3,2,0,1:T(8,128)(2,1)S(1)}, u32[]{:S(2)}, u32[]{:S(2)}) collective-permute-start(bf16[1,1,8,7168]{3,2,0,1:T(8,128)(2,1)S(1)} %constant_dynamic-slice_fusion.14), channel_id=1, source_target_pairs={{0,2},{2,4},{4,6},{6,8},{8,10},{10,12},{12,14},{14,16},{16,18},{18... | collective-permute-start | bytes 344072 | tf_op jit(solution)/shard_map/ppermute | solution.py:25
  39.8 9.2 %collective-permute-start.1 = (bf16[1,1,8,7168]{3,2,0,1:T(8,128)(2,1)S(1)}, bf16[1,1,8,7168]{3,2,0,1:T(8,128)(2,1)S(1)}, u32[]{:S(2)}, u32[]{:S(2)}) collective-permute-start(bf16[1,1,8,7168]{3,2,0,1:T(8,128)(2,1)S(1)} %get-tuple-element.18), channel_id=1, source_target_pairs={{0,4},{2,6},{4,8},{6,10},{8,12},{10,14},{12,16},{14,18},{16,20},{1... | collective-permute-start | bytes 344072 | tf_op jit(solution)/shard_map/ppermute | solution.py:25
  39.8 74.1 %collective-permute-start.14 = (bf16[1,1,8,7168]{3,2,0,1:T(8,128)(2,1)S(1)}, bf16[1,1,8,7168]{3,2,0,1:T(8,128)(2,1)S(1)}, u32[]{:S(2)}, u32[]{:S(2)}) collective-permute-start(bf16[1,1,8,7168]{3,2,0,1:T(8,128)(2,1)S(1)} %get-tuple-element.5), channel_id=1, source_target_pairs={{0,30},{2,0},{4,2},{6,4},{8,6},{10,8},{12,10},{14,12},{16,14},{18,... | collective-permute-start | bytes 344072 | tf_op jit(solution)/shard_map/ppermute | solution.py:25
  42.1 71.8 %collective-permute-start.13 = (bf16[1,1,8,7168]{3,2,0,1:T(8,128)(2,1)S(1)}, bf16[1,1,8,7168]{3,2,0,1:T(8,128)(2,1)S(1)}, u32[]{:S(2)}, u32[]{:S(2)}) collective-permute-start(bf16[1,1,8,7168]{3,2,0,1:T(8,128)(2,1)S(1)} %get-tuple-element.6), channel_id=1, source_target_pairs={{0,28},{2,30},{4,0},{6,2},{8,4},{10,6},{12,8},{14,10},{16,12},{18,... | collective-permute-start | bytes 344072 | tf_op jit(solution)/shard_map/ppermute | solution.py:25
  44.6 69.3 %collective-permute-start.12 = (bf16[1,1,8,7168]{3,2,0,1:T(8,128)(2,1)S(1)}, bf16[1,1,8,7168]{3,2,0,1:T(8,128)(2,1)S(1)}, u32[]{:S(2)}, u32[]{:S(2)}) collective-permute-start(bf16[1,1,8,7168]{3,2,0,1:T(8,128)(2,1)S(1)} %get-tuple-element.7), channel_id=1, source_target_pairs={{0,26},{2,28},{4,30},{6,0},{8,2},{10,4},{12,6},{14,8},{16,10},{18,... | collective-permute-start | bytes 344072 | tf_op jit(solution)/shard_map/ppermute | solution.py:25
  45.9 67.8 %collective-permute-start.11 = (bf16[1,1,8,7168]{3,2,0,1:T(8,128)(2,1)S(1)}, bf16[1,1,8,7168]{3,2,0,1:T(8,128)(2,1)S(1)}, u32[]{:S(2)}, u32[]{:S(2)}) collective-permute-start(bf16[1,1,8,7168]{3,2,0,1:T(8,128)(2,1)S(1)} %get-tuple-element.8), channel_id=1, source_target_pairs={{0,24},{2,26},{4,28},{6,30},{8,0},{10,2},{12,4},{14,6},{16,8},{18,... | collective-permute-start | bytes 344072 | tf_op jit(solution)/shard_map/ppermute | solution.py:25
  49.1 7.5 %collective-permute-start.2 = (bf16[1,1,8,7168]{3,2,0,1:T(8,128)(2,1)S(1)}, bf16[1,1,8,7168]{3,2,0,1:T(8,128)(2,1)S(1)}, u32[]{:S(2)}, u32[]{:S(2)}) collective-permute-start(bf16[1,1,8,7168]{3,2,0,1:T(8,128)(2,1)S(1)} %get-tuple-element.17), channel_id=1, source_target_pairs={{0,6},{2,8},{4,10},{6,12},{8,14},{10,16},{12,18},{14,20},{16,22},{... | collective-permute-start | bytes 344072 | tf_op jit(solution)/shard_map/ppermute | solution.py:25
  56.6 6.8 %collective-permute-start.3 = (bf16[1,1,8,7168]{3,2,0,1:T(8,128)(2,1)}, bf16[1,1,8,7168]{3,2,0,1:T(8,128)(2,1)S(1)}, u32[]{:S(2)}, u32[]{:S(2)}) collective-permute-start(bf16[1,1,8,7168]{3,2,0,1:T(8,128)(2,1)} %get-tuple-element.16), channel_id=1, source_target_pairs={{0,8},{2,10},{4,12},{6,14},{8,16},{10,18},{12,20},{14,22},{16,24},... | collective-permute-start | bytes 344072 | tf_op jit(solution)/shard_map/ppermute | solution.py:25
  63.4 10.2 %collective-permute-start.4 = (bf16[1,1,8,7168]{3,2,0,1:T(8,128)(2,1)}, bf16[1,1,8,7168]{3,2,0,1:T(8,128)(2,1)S(1)}, u32[]{:S(2)}, u32[]{:S(2)}) collective-permute-start(bf16[1,1,8,7168]{3,2,0,1:T(8,128)(2,1)} %get-tuple-element.15), channel_id=1, source_target_pairs={{0,10},{2,12},{4,14},{6,16},{8,18},{10,20},{12,22},{14,24},{16,26}... | collective-permute-start | bytes 344072 | tf_op jit(solution)/shard_map/ppermute | solution.py:25
  73.6 6.8 %collective-permute-start.5 = (bf16[1,1,8,7168]{3,2,0,1:T(8,128)(2,1)}, bf16[1,1,8,7168]{3,2,0,1:T(8,128)(2,1)S(1)}, u32[]{:S(2)}, u32[]{:S(2)}) collective-permute-start(bf16[1,1,8,7168]{3,2,0,1:T(8,128)(2,1)} %get-tuple-element.14), channel_id=1, source_target_pairs={{0,12},{2,14},{4,16},{6,18},{8,20},{10,22},{12,24},{14,26},{16,28}... | collective-permute-start | bytes 344072 | tf_op jit(solution)/shard_map/ppermute | solution.py:25
  80.4 7.8 %collective-permute-start.6 = (bf16[1,1,8,7168]{3,2,0,1:T(8,128)(2,1)}, bf16[1,1,8,7168]{3,2,0,1:T(8,128)(2,1)S(1)}, u32[]{:S(2)}, u32[]{:S(2)}) collective-permute-start(bf16[1,1,8,7168]{3,2,0,1:T(8,128)(2,1)} %get-tuple-element.13), channel_id=1, source_target_pairs={{0,14},{2,16},{4,18},{6,20},{8,22},{10,24},{12,26},{14,28},{16,30}... | collective-permute-start | bytes 344072 | tf_op jit(solution)/shard_map/ppermute | solution.py:25
  88.2 7.1 %collective-permute-start.7 = (bf16[1,1,8,7168]{3,2,0,1:T(8,128)(2,1)S(1)}, bf16[1,1,8,7168]{3,2,0,1:T(8,128)(2,1)S(1)}, u32[]{:S(2)}, u32[]{:S(2)}) collective-permute-start(bf16[1,1,8,7168]{3,2,0,1:T(8,128)(2,1)S(1)} %get-tuple-element.12), channel_id=1, source_target_pairs={{0,16},{2,18},{4,20},{6,22},{8,24},{10,26},{12,28},{14,30},{16,0},... | collective-permute-start | bytes 344072 | tf_op jit(solution)/shard_map/ppermute | solution.py:25
  95.3 6.8 %collective-permute-start.8 = (bf16[1,1,8,7168]{3,2,0,1:T(8,128)(2,1)}, bf16[1,1,8,7168]{3,2,0,1:T(8,128)(2,1)S(1)}, u32[]{:S(2)}, u32[]{:S(2)}) collective-permute-start(bf16[1,1,8,7168]{3,2,0,1:T(8,128)(2,1)} %get-tuple-element.11), channel_id=1, source_target_pairs={{0,18},{2,20},{4,22},{6,24},{8,26},{10,28},{12,30},{14,0},{16,2},{... | collective-permute-start | bytes 344072 | tf_op jit(solution)/shard_map/ppermute | solution.py:25
  102.1 5.7 %collective-permute-start.9 = (bf16[1,1,8,7168]{3,2,0,1:T(8,128)(2,1)S(1)}, bf16[1,1,8,7168]{3,2,0,1:T(8,128)(2,1)S(1)}, u32[]{:S(2)}, u32[]{:S(2)}) collective-permute-start(bf16[1,1,8,7168]{3,2,0,1:T(8,128)(2,1)S(1)} %get-tuple-element.10), channel_id=1, source_target_pairs={{0,20},{2,22},{4,24},{6,26},{8,28},{10,30},{12,0},{14,2},{16,4},{1... | collective-permute-start | bytes 344072 | tf_op jit(solution)/shard_map/ppermute | solution.py:25
  107.8 6.0 %collective-permute-start.10 = (bf16[1,1,8,7168]{3,2,0,1:T(8,128)(2,1)S(1)}, bf16[1,1,8,7168]{3,2,0,1:T(8,128)(2,1)S(1)}, u32[]{:S(2)}, u32[]{:S(2)}) collective-permute-start(bf16[1,1,8,7168]{3,2,0,1:T(8,128)(2,1)S(1)} %get-tuple-element.9), channel_id=1, source_target_pairs={{0,22},{2,24},{4,26},{6,28},{8,30},{10,0},{12,2},{14,4},{16,6},{18... | collective-permute-start | bytes 344072 | tf_op jit(solution)/shard_map/ppermute | solution.py:25
  113.8 6.5 %slice-start = ((s8[7340032]{0:T(1024)(128)(4,1)}), s8[4194304]{0:T(1024)(128)(4,1)S(1)}, s32[]{:S(2)}) async-start(s8[7340032]{0:T(1024)(128)(4,1)} %bitcast.32), calls=%async_computation.2 | async-start | bytes 8388608
  113.9 6.4 %slice-start.1 = ((s8[7340032]{0:T(1024)(128)(4,1)}), s8[3145728]{0:T(1024)(128)(4,1)S(1)}, s32[]{:S(2)}) async-start(s8[7340032]{0:T(1024)(128)(4,1)} %bitcast.32), calls=%async_computation.3 | async-start | bytes 6291456
  122.4 9.4 %copy-start = (s32[128,8]{0,1:T(8,128)S(1)}, s32[128,8]{0,1:T(8,128)}, u32[]{:S(2)}) copy-start(s32[128,8]{0,1:T(8,128)} %param.6) | copy-start | bytes 12292
  122.4 9.4 %copy-start.1 = (f32[128,8]{0,1:T(8,128)S(1)}, f32[128,8]{0,1:T(8,128)}, u32[]{:S(2)}) copy-start(f32[128,8]{0,1:T(8,128)} %param.7) | copy-start | bytes 12292
  122.4 31.6 %all-to-all-start = ((bf16[16,8,3584]{2,1,0:T(8,128)(2,1)}), bf16[16,8,3584]{2,1,0:T(8,128)(2,1)S(1)}, u32[]{:S(2)}, u32[]{:S(2)}) async-start(bf16[16,8,3584]{2,1,0:T(8,128)(2,1)} %fusion.7), calls=%async_computation | async-start | bytes 1835008 | tf_op jit(solution)/shard_map/all_to_all | solution.py:84
Sparse Core Ops, SparseCore 0:
  8.9 12.8 all-gather.2
